TPU v7x, 256 devices: a whole 4x4x8 slice. The times are simulated.
256 devices in a mesh: lx: 8 (over z), ly: 8 (over x, y_lo), blk: 4 (over y_hi, core).
Axes of the slice: x: 4, y: 4 (y_hi: 2, y_lo: 2; y = y_hi * 2 + y_lo), z: 8, core: 2. Of those that a mesh axis runs over, the one named last changes fastest.
Arguments:
- block_vectors: float32 [32, 1024, 2048], P('blk', 'lx', 'ly'), may hold values from -6 to 6
- search_vectors: float32 [256, 1024, 2048], P('blk', 'lx', 'ly'), may hold values from -6 to 6
- onsite_energy: float32 [1024, 2048], P('lx', 'ly'), may hold values from -1 to 1
- site_mask: int32 [1024, 2048], P('lx', 'ly'), may hold values 0 or 1
- filter_coefs: float32 [5], replicated, may hold values from -1 to 1
Outputs:
- projected: float32 [2, 32, 256], P(None, None, 'blk')
Inputs may be any that keep to these rules, and one draw needn't show every extreme that they name: `site_mask`: 1 marks a present site, 0 a vacancy.
All inputs are finite; a program needn't handle non-finite values. No bound on the sum of `site_mask` on one device may be relied on, other than what follows from the above.
Results may differ from a plain program's by a relative error of at most 0.00016.
Values sent between devices are 32-bit elements; how exact they have to be, the bound alone decides.
No kernel may reach another device: no remote copies, remote signals or barrier semaphores. Data moves between devices by JAX's collectives and lax.ppermute only.
A program may use at most 64 MiB of HBM per device.

v0:
```python
import math
import jax
import jax.numpy as jnp
from jax import lax
from jax.sharding import PartitionSpec as P


def extended(block, sides, width):
    for axis, dim in sides:
        count = lax.axis_size(axis)
        forward = [(i, i + 1) for i in range(count - 1)]
        backward = [(target, source) for source, target in forward]
        low = lax.ppermute(
            lax.slice_in_dim(block, block.shape[dim] - width, None, axis=dim), axis, forward
        )
        high = lax.ppermute(lax.slice_in_dim(block, 0, width, axis=dim), axis, backward)
        block = jnp.concatenate([low, block, high], axis=dim)
    return block


def scaled_step(padded, onsite, present):
    nrows, ncols = onsite.shape
    row_index = lax.broadcasted_iota(jnp.int32, (nrows, ncols), 0)
    col_index = lax.broadcasted_iota(jnp.int32, (nrows, ncols), 1)
    even_sites = (row_index + col_index) % 2 == 0
    centre = padded[..., 1:-1, 1:-1]
    left_side = padded[..., 1:-1, :-2]
    right_side = padded[..., 1:-1, 2:]
    upper_side = padded[..., :-2, 1:-1]
    lower_side = padded[..., 2:, 1:-1]
    vertical = jnp.where(even_sites, lower_side, upper_side)
    return present * (onsite * centre - (left_side + right_side + vertical)) * 0.25


def gram_rows(stacked, search_vectors):
    stacks, members, nrows, ncols = stacked.shape
    flat = stacked.reshape(stacks * members, nrows * ncols)
    search_flat = search_vectors.reshape(search_vectors.shape[0], nrows * ncols)
    result = lax.dot_general(
        flat,
        search_flat,
        (((1,), (1,)), ((), ())),
        precision=lax.Precision.HIGHEST,
        preferred_element_type=jnp.float32,
    )
    return result.reshape(stacks, members, search_vectors.shape[0])


def shards(block_vectors, search_vectors, onsite_energy, site_mask, filter_coefs):
    present = site_mask.astype(jnp.float32)
    current = block_vectors * present
    filtered = filter_coefs[0] * current
    degree = filter_coefs.shape[0] - 1
    before = current
    for order in range(1, degree + 1):
        padded_field = extended(current, (("lx", 1), ("ly", 2)), 1)
        image = scaled_step(padded_field, onsite_energy, present)
        following = image if order == 1 else 2.0 * image - before
        before, current = (current, following)
        filtered = filtered + filter_coefs[order] * current
    nrows, ncols = onsite_energy.shape
    scale_factor = 1.0 / math.sqrt(nrows * ncols * lax.axis_size("lx") * lax.axis_size("ly"))
    padded_field = extended(filtered, (("lx", 1), ("ly", 2)), 1)
    image = scaled_step(padded_field, onsite_energy, present)
    paired = jnp.stack([filtered, image])
    partial_gram = gram_rows(lax.all_gather(paired, "blk", axis=1, tiled=True), search_vectors)
    total = lax.psum(partial_gram, ("lx", "ly"))
    return total * scale_factor


def solution(mesh):
    placed = (P("blk", "lx", "ly"), P("blk", "lx", "ly"), P("lx", "ly"), P("lx", "ly"), P())
    return jax.shard_map(
        shards, mesh=mesh, in_specs=placed, out_specs=P(None, None, "blk"), check_vma=False
    )
```

profile of v0, /device:TPU:16, one launch (start us, length us, event | category | flops | bytes accessed | tf_op | source)
XLA Modules:
  0.0 537.4 jit_solution(5126460402475514423)
XLA Ops:
  7.5 1.8 copy_multiply_fusion
  10.6 4.5 collective-permute-start
  15.2 1.3 collective-permute-done
  18.8 4.5 collective-permute-start.2
  23.4 1.3 collective-permute-done.2
  27.1 1.9 broadcast_multiply_fusion
  30.3 4.8 collective-permute-start.4
  35.2 1.3 collective-permute-done.4
  37.6 1.4 copy.13
  40.6 4.8 collective-permute-start.6
  49.2 2.6 fusion.34
  53.1 4.8 collective-permute-start.8
  58.0 1.3 collective-permute-done.8
  60.4 1.4 copy.17
  61.8 5.0 collective-permute-start.10
  68.8 5.0 collective-permute-done.11
  75.0 1.8 fusion.27
  78.1 4.9 collective-permute-start.12
  83.1 1.3 collective-permute-done.12
  85.5 1.4 copy.21
  88.5 5.4 %collective-permute-start.14 = (f32[8,130,1]{1,0,2:T(8,128)S(1)}, f32[8,130,1]{1,0,2:T(8,128)S(1)}, u32[]{:S(2)}, u32[]{:S(2)}) collective-permute-start(f32[8,130,1]{1,0,2:T(8,128)S(1)} %copy.21), channel_id=1, source_target_pairs={{0,4},{4,8},{8,12},{12,16},{16,20},{20,24},{24,28},{1,5},{5,9},{9,... | collective-permute-start | bytes 12488 | tf_op jit(solution)/shard_map/ppermute | solution.py:13
  97.7 8.3 %fusion.20 = f32[8,128,256]{2,0,1:T(8,128)S(1)} fusion(f32[8,128,256]{2,0,1:T(8,128)S(1)} %fusion.34, f32[8,128,256]{2,0,1:T(8,128)} %copy-done, f32[8,1,256]{2,0,1:T(8,128)S(1)} %collective-permute-done.12, f32[8,1,256]{2,0,1:T(8,128)S(1)} %collective-permute-done.13, f32[8,130,1]{2,0,1:T(8,128)} %copy.24, f32[8,130,1]{2,0,1:T(8,128)} %copy.22, ...), kind=kLoop, calls=%fused_computation.33 | loop fusion | flops 6815744 | bytes 5562516 | tf_op jit(solution)/shard_map/add | solution.py:60
  107.3 6.0 %collective-permute-start.16 = (f32[8,1,256]{2,0,1:T(8,128)S(1)}, f32[8,1,256]{2,0,1:T(8,128)S(1)}, u32[]{:S(2)}, u32[]{:S(2)}) collective-permute-start(f32[8,1,256]{2,0,1:T(8,128)S(1)} %get-tuple-element.18), channel_id=1, source_target_pairs={{0,32},{32,64},{64,96},{96,128},{128,160},{160,192},{192,224},{1,3... | collective-permute-start | bytes 24584 | tf_op jit(solution)/shard_map/ppermute | solution.py:13
  113.3 1.3 collective-permute-done.16
  115.3 4.8 collective-permute-start.18
  120.5 1.5 collective-permute-start.19
  122.4 4.8 collective-permute-done.19
  128.4 1.8 fusion.11
  130.2 1.5 pad_maximum_fusion
  131.7 71.7 %all-gather.2.cloned.1.call-done = f32[2,32,128,256]{3,1,2,0:T(8,128)} async-done(((f32[2,8,128,256]{3,1,2,0:T(8,128)}), f32[2,32,128,256]{3,1,2,0:T(8,128)}) %all-gather.2.cloned.1.call-update) | async-done | bytes 8388624 | tf_op jit(solution)/shard_map/all_gather | solution.py:66
  203.4 16.7 %fusion.3 = f32[2,32,64]{2,1,0:T(8,128)S(1)} fusion(f32[2,32,128,256]{3,1,2,0:T(8,128)} %all-gather.2.cloned.1.call-done, f32[64,128,256]{2,1,0:T(8,128)} %param.6), kind=kOutput, calls=%fused_computation.4 | convolution fusion | flops 1610612736 | bytes 16793600 | tf_op jit(solution)/shard_map/dot_general | solution.py:39
  220.0 309.9 %psum.7 = f32[2,32,64]{2,1,0:T(8,128)S(1)} all-reduce(f32[2,32,64]{2,1,0:T(8,128)S(1)} %fusion.3), channel_id=1, replica_groups=mesh['lx'=8,'ly'=8,'blk'=4] {'lx','ly'}, use_global_device_ids=true, to_apply=%region_0.1 | all-reduce | flops 4096 | bytes 32768 | tf_op jit(solution)/shard_map/psum | solution.py:67
  (66 shorter events, 31.8 us)
Async XLA Ops:
  6.5 196.8 %all-gather.2.cloned.1.call-start = ((), (), s32[]{:S(2)}) async-start(), calls=%async_computation | async-start | bytes 10485760 | tf_op jit(solution)/shard_map/all_gather | solution.py:66
  9.3 5.9 %collective-permute-start.1 = (f32[8,1,256]{2,0,1:T(8,128)S(1)}, f32[8,1,256]{2,0,1:T(8,128)S(1)}, u32[]{:S(2)}, u32[]{:S(2)}) collective-permute-start(f32[8,1,256]{2,0,1:T(8,128)S(1)} %get-tuple-element.25), channel_id=1, source_target_pairs={{32,0},{64,32},{96,64},{128,96},{160,128},{192,160},{224,192},{33,... | collective-permute-start | bytes 24584 | tf_op jit(solution)/shard_map/ppermute | solution.py:16
  10.6 5.9 %collective-permute-start = (f32[8,1,256]{2,0,1:T(8,128)S(1)}, f32[8,1,256]{2,0,1:T(8,128)S(1)}, u32[]{:S(2)}, u32[]{:S(2)}) collective-permute-start(f32[8,1,256]{2,0,1:T(8,128)S(1)} %get-tuple-element.26), channel_id=1, source_target_pairs={{0,32},{32,64},{64,96},{96,128},{128,160},{160,192},{192,224},{1,3... | collective-permute-start | bytes 24584 | tf_op jit(solution)/shard_map/ppermute | solution.py:13
  16.8 10.3 %copy-start.1 = (f32[128,256]{1,0:T(8,128)S(1)}, f32[128,256]{1,0:T(8,128)}, u32[]{:S(2)}) copy-start(f32[128,256]{1,0:T(8,128)} %param.7) | copy-start | bytes 393220
  17.5 8.4 %collective-permute-start.3 = (f32[8,130,1]{1,0,2:T(8,128)S(1)}, f32[8,130,1]{1,0,2:T(8,128)S(1)}, u32[]{:S(2)}, u32[]{:S(2)}) collective-permute-start(f32[8,130,1]{1,0,2:T(8,128)S(1)} %copy.11), channel_id=1, source_target_pairs={{4,0},{8,4},{12,8},{16,12},{20,16},{24,20},{28,24},{5,1},{9,5},{13... | collective-permute-start | bytes 12488 | tf_op jit(solution)/shard_map/ppermute | solution.py:16
  18.8 5.9 %collective-permute-start.2 = (f32[8,130,1]{1,0,2:T(8,128)S(1)}, f32[8,130,1]{1,0,2:T(8,128)S(1)}, u32[]{:S(2)}, u32[]{:S(2)}) collective-permute-start(f32[8,130,1]{1,0,2:T(8,128)S(1)} %copy.9), channel_id=1, source_target_pairs={{0,4},{4,8},{8,12},{12,16},{16,20},{20,24},{24,28},{1,5},{5,9},{9,... | collective-permute-start | bytes 12488 | tf_op jit(solution)/shard_map/ppermute | solution.py:13
  29.0 6.1 %collective-permute-start.5 = (f32[8,1,256]{2,0,1:T(8,128)S(1)}, f32[8,1,256]{2,0,1:T(8,128)S(1)}, u32[]{:S(2)}, u32[]{:S(2)}) collective-permute-start(f32[8,1,256]{2,0,1:T(8,128)S(1)} %get-tuple-element.23), channel_id=1, source_target_pairs={{32,0},{64,32},{96,64},{128,96},{160,128},{192,160},{224,192},{33,... | collective-permute-start | bytes 24584 | tf_op jit(solution)/shard_map/ppermute | solution.py:16
  30.3 6.2 %collective-permute-start.4 = (f32[8,1,256]{2,0,1:T(8,128)S(1)}, f32[8,1,256]{2,0,1:T(8,128)S(1)}, u32[]{:S(2)}, u32[]{:S(2)}) collective-permute-start(f32[8,1,256]{2,0,1:T(8,128)S(1)} %get-tuple-element.24), channel_id=1, source_target_pairs={{0,32},{32,64},{64,96},{96,128},{128,160},{160,192},{192,224},{1,3... | collective-permute-start | bytes 24584 | tf_op jit(solution)/shard_map/ppermute | solution.py:13
  39.3 8.7 %collective-permute-start.7 = (f32[8,130,1]{1,0,2:T(8,128)S(1)}, f32[8,130,1]{1,0,2:T(8,128)S(1)}, u32[]{:S(2)}, u32[]{:S(2)}) collective-permute-start(f32[8,130,1]{1,0,2:T(8,128)S(1)} %copy.15), channel_id=1, source_target_pairs={{4,0},{8,4},{12,8},{16,12},{20,16},{24,20},{28,24},{5,1},{9,5},{13... | collective-permute-start | bytes 12488 | tf_op jit(solution)/shard_map/ppermute | solution.py:16
  40.6 6.2 %collective-permute-start.6 = (f32[8,130,1]{1,0,2:T(8,128)S(1)}, f32[8,130,1]{1,0,2:T(8,128)S(1)}, u32[]{:S(2)}, u32[]{:S(2)}) collective-permute-start(f32[8,130,1]{1,0,2:T(8,128)S(1)} %copy.13), channel_id=1, source_target_pairs={{0,4},{4,8},{8,12},{12,16},{16,20},{20,24},{24,28},{1,5},{5,9},{9,... | collective-permute-start | bytes 12488 | tf_op jit(solution)/shard_map/ppermute | solution.py:13
  51.8 6.1 %collective-permute-start.9 = (f32[8,1,256]{2,0,1:T(8,128)S(1)}, f32[8,1,256]{2,0,1:T(8,128)S(1)}, u32[]{:S(2)}, u32[]{:S(2)}) collective-permute-start(f32[8,1,256]{2,0,1:T(8,128)S(1)} %get-tuple-element.21), channel_id=1, source_target_pairs={{32,0},{64,32},{96,64},{128,96},{160,128},{192,160},{224,192},{33,... | collective-permute-start | bytes 24584 | tf_op jit(solution)/shard_map/ppermute | solution.py:16
  53.1 6.2 %collective-permute-start.8 = (f32[8,1,256]{2,0,1:T(8,128)S(1)}, f32[8,1,256]{2,0,1:T(8,128)S(1)}, u32[]{:S(2)}, u32[]{:S(2)}) collective-permute-start(f32[8,1,256]{2,0,1:T(8,128)S(1)} %get-tuple-element.22), channel_id=1, source_target_pairs={{0,32},{32,64},{64,96},{96,128},{128,160},{160,192},{192,224},{1,3... | collective-permute-start | bytes 24584 | tf_op jit(solution)/shard_map/ppermute | solution.py:13
  61.8 6.6 %collective-permute-start.10 = (f32[8,130,1]{1,0,2:T(8,128)S(1)}, f32[8,130,1]{1,0,2:T(8,128)S(1)}, u32[]{:S(2)}, u32[]{:S(2)}) collective-permute-start(f32[8,130,1]{1,0,2:T(8,128)S(1)} %copy.17), channel_id=1, source_target_pairs={{0,4},{4,8},{8,12},{12,16},{16,20},{20,24},{24,28},{1,5},{5,9},{9,... | collective-permute-start | bytes 12488 | tf_op jit(solution)/shard_map/ppermute | solution.py:13
  67.1 6.7 %collective-permute-start.11 = (f32[8,130,1]{1,0,2:T(8,128)S(1)}, f32[8,130,1]{1,0,2:T(8,128)S(1)}, u32[]{:S(2)}, u32[]{:S(2)}) collective-permute-start(f32[8,130,1]{1,0,2:T(8,128)S(1)} %copy.19), channel_id=1, source_target_pairs={{4,0},{8,4},{12,8},{16,12},{20,16},{24,20},{28,24},{5,1},{9,5},{13... | collective-permute-start | bytes 12488 | tf_op jit(solution)/shard_map/ppermute | solution.py:16
  76.8 7.7 %copy-start = (f32[8,128,256]{2,0,1:T(8,128)}, f32[8,128,256]{2,0,1:T(8,128)S(1)}, u32[]{:S(2)}) copy-start(f32[8,128,256]{2,0,1:T(8,128)S(1)} %fusion.27) | copy-start | bytes 3145732
  76.8 6.2 %collective-permute-start.13 = (f32[8,1,256]{2,0,1:T(8,128)S(1)}, f32[8,1,256]{2,0,1:T(8,128)S(1)}, u32[]{:S(2)}, u32[]{:S(2)}) collective-permute-start(f32[8,1,256]{2,0,1:T(8,128)S(1)} %get-tuple-element.19), channel_id=1, source_target_pairs={{32,0},{64,32},{96,64},{128,96},{160,128},{192,160},{224,192},{33,... | collective-permute-start | bytes 24584 | tf_op jit(solution)/shard_map/ppermute | solution.py:16
  78.1 6.3 %collective-permute-start.12 = (f32[8,1,256]{2,0,1:T(8,128)S(1)}, f32[8,1,256]{2,0,1:T(8,128)S(1)}, u32[]{:S(2)}, u32[]{:S(2)}) collective-permute-start(f32[8,1,256]{2,0,1:T(8,128)S(1)} %get-tuple-element.20), channel_id=1, source_target_pairs={{0,32},{32,64},{64,96},{96,128},{128,160},{160,192},{192,224},{1,3... | collective-permute-start | bytes 24584 | tf_op jit(solution)/shard_map/ppermute | solution.py:13
  85.5 8.5 %copy-start.2 = (f32[5]{0:T(128)S(1)}, f32[5]{0:T(128)}, u32[]{:S(2)}) copy-start(f32[5]{0:T(128)} %param.9) | copy-start | bytes 64
  87.2 9.3 %collective-permute-start.15 = (f32[8,130,1]{1,0,2:T(8,128)S(1)}, f32[8,130,1]{1,0,2:T(8,128)S(1)}, u32[]{:S(2)}, u32[]{:S(2)}) collective-permute-start(f32[8,130,1]{1,0,2:T(8,128)S(1)} %copy.23), channel_id=1, source_target_pairs={{4,0},{8,4},{12,8},{16,12},{20,16},{24,20},{28,24},{5,1},{9,5},{13... | collective-permute-start | bytes 12488 | tf_op jit(solution)/shard_map/ppermute | solution.py:16
  88.5 6.8 %collective-permute-start.14 = (f32[8,130,1]{1,0,2:T(8,128)S(1)}, f32[8,130,1]{1,0,2:T(8,128)S(1)}, u32[]{:S(2)}, u32[]{:S(2)}) collective-permute-start(f32[8,130,1]{1,0,2:T(8,128)S(1)} %copy.21), channel_id=1, source_target_pairs={{0,4},{4,8},{8,12},{12,16},{16,20},{20,24},{24,28},{1,5},{5,9},{9,... | collective-permute-start | bytes 12488 | tf_op jit(solution)/shard_map/ppermute | solution.py:13
  106.0 7.3 %collective-permute-start.17 = (f32[8,1,256]{2,0,1:T(8,128)S(1)}, f32[8,1,256]{2,0,1:T(8,128)S(1)}, u32[]{:S(2)}, u32[]{:S(2)}) collective-permute-start(f32[8,1,256]{2,0,1:T(8,128)S(1)} %get-tuple-element.17), channel_id=1, source_target_pairs={{32,0},{64,32},{96,64},{128,96},{160,128},{192,160},{224,192},{33,... | collective-permute-start | bytes 24584 | tf_op jit(solution)/shard_map/ppermute | solution.py:16
  107.3 7.4 %collective-permute-start.16 = (f32[8,1,256]{2,0,1:T(8,128)S(1)}, f32[8,1,256]{2,0,1:T(8,128)S(1)}, u32[]{:S(2)}, u32[]{:S(2)}) collective-permute-start(f32[8,1,256]{2,0,1:T(8,128)S(1)} %get-tuple-element.18), channel_id=1, source_target_pairs={{0,32},{32,64},{64,96},{96,128},{128,160},{160,192},{192,224},{1,3... | collective-permute-start | bytes 24584 | tf_op jit(solution)/shard_map/ppermute | solution.py:13
  115.3 6.7 %collective-permute-start.18 = (f32[8,130,1]{1,0,2:T(8,128)S(1)}, f32[8,130,1]{1,0,2:T(8,128)S(1)}, u32[]{:S(2)}, u32[]{:S(2)}) collective-permute-start(f32[8,130,1]{1,0,2:T(8,128)S(1)} %copy.25), channel_id=1, source_target_pairs={{0,4},{4,8},{8,12},{12,16},{16,20},{20,24},{24,28},{1,5},{5,9},{9,... | collective-permute-start | bytes 12488 | tf_op jit(solution)/shard_map/ppermute | solution.py:13
  120.5 6.7 %collective-permute-start.19 = (f32[8,130,1]{1,0,2:T(8,128)S(1)}, f32[8,130,1]{1,0,2:T(8,128)S(1)}, u32[]{:S(2)}, u32[]{:S(2)}) collective-permute-start(f32[8,130,1]{1,0,2:T(8,128)S(1)} %copy.27), channel_id=1, source_target_pairs={{4,0},{8,4},{12,8},{16,12},{20,16},{24,20},{28,24},{5,1},{9,5},{13... | collective-permute-start | bytes 12488 | tf_op jit(solution)/shard_map/ppermute | solution.py:16
Sparse Core Ops, SparseCore 0:
  131.8 71.4 all-gather.1
where the time goes:
time: 538 us; the launch traced here: 537 us
  blocking collectives  310 us (58%)
  waiting for transfers between devices  90.3 us (17%)
  starting transfers between devices  62.9 us (12%)
  other arithmetic  22.4 us (4%)
  local copies, waits for them, and re-layouts  20.9 us (4%)
  matrix products  16.7 us (3%)
  between operations  14.3 us (3%)
    psum x1, blocking collectives, shards(): total = lax.psum(partial_gram, ('lx', 'ly'))  310 us
    all_gather x1, waiting for transfers between devices, shards(): lax.all_gather(paired, 'blk', axis=1, tiled=True)  71.7 us
    ppermute x10, starting transfers between devices, extended(): lax.ppermute(lax.slice_in_dim(block, block.shape[dim] - width, None, axis...  49.7 us
    dot_general x1, matrix products, gram_rows(): lax.dot_general(flat, search_flat, (((1,), (1,)), ((), ())), precision=la...  16.7 us
    ppermute x10, starting transfers between devices, extended(): lax.ppermute(lax.slice_in_dim(block, 0, width, axis=dim), axis, backward)  13.1 us
  transfers between devices with their start and end apart: 21, of which 11 were waited for; matrix products, arithmetic and copies ran while one was open for 1% of the time, Pallas kernels for 0%

commit v1 on v0

--- a/solution.py
+++ b/solution.py
@@ -63,7 +63,12 @@
     padded_field = extended(filtered, (("lx", 1), ("ly", 2)), 1)
     image = scaled_step(padded_field, onsite_energy, present)
     paired = jnp.stack([filtered, image])
-    partial_gram = gram_rows(lax.all_gather(paired, "blk", axis=1, tiled=True), search_vectors)
+    partial_gram = gram_rows(
+        jnp.concatenate(
+            lax.all_to_all(jnp.stack([paired] * lax.axis_size("blk")), "blk", 0, 0), axis=1
+        ),
+        search_vectors,
+    )
     total = lax.psum(partial_gram, ("lx", "ly"))
     return total * scale_factor
 

time: 538 us -> 555 us (1.032)
  local copies, waits for them, and re-layouts: 20.9 us -> 40.1 us
  between operations: 14.3 us -> 0.97 us
  waiting for transfers between devices: 90.3 us -> 101 us
  matrix products: 16.7 us -> 6.76 us
  starting transfers between devices: 62.9 us -> 69.1 us
    all_to_all x0 -> x1, waiting for transfers between devices: none -> 82.1 us  [shards(): lax.all_to_all(jnp.stack([paired] * lax.axis_size('blk')), 'blk', 0, 0)]
    all_gather x1 -> x0, waiting for transfers between devices: 71.7 us -> none  [shards(): lax.all_gather(paired, 'blk', axis=1, tiled=True)]
    reshape x0 -> x2, local copies, waits for them, and re-layouts: none -> 13.6 us  [the longest x1 9.45 us: gram_rows(): search_flat = search_vectors.reshape(search_vectors.shape[0], nrows * ncols)]
    dot_general x1, matrix products: 16.7 us -> 6.76 us  [gram_rows(): lax.dot_general(flat, search_flat, (((1,), (1,)), ((), ())), precision=la...]
    all_to_all x0 -> x1, starting transfers between devices: none -> 6.24 us  [shards(): lax.all_to_all(jnp.stack([paired] * lax.axis_size('blk')), 'blk', 0, 0)]
  transfers between devices with their start and end apart: 21 -> 21, of which waited for: 11 -> 11; matrix products, arithmetic and copies ran while one was open for 1% -> 3% of each run, Pallas kernels for 0% -> 0%
where the time goes in v1:
time: 555 us; the launch traced here: 553 us
  blocking collectives  314 us (57%)
  waiting for transfers between devices  101 us (18%)
  starting transfers between devices  69.1 us (12%)
  local copies, waits for them, and re-layouts  40.1 us (7%)
  other arithmetic  21 us (4%)
  matrix products  6.76 us (1%)
    psum x1, blocking collectives, shards(): total = lax.psum(partial_gram, ('lx', 'ly'))  314 us
    all_to_all x1, waiting for transfers between devices, shards(): lax.all_to_all(jnp.stack([paired] * lax.axis_size('blk')), 'blk', 0, 0)  82.1 us
    ppermute x10, starting transfers between devices, extended(): lax.ppermute(lax.slice_in_dim(block, block.shape[dim] - width, None, axis...  49.7 us
    ppermute x10, starting transfers between devices, extended(): lax.ppermute(lax.slice_in_dim(block, 0, width, axis=dim), axis, backward)  13.1 us
  transfers between devices with their start and end apart: 21, of which 11 were waited for; matrix products, arithmetic and copies ran while one was open for 3% of the time, Pallas kernels for 0%

profile of v1, /device:TPU:16, one launch (start us, length us, event | category | flops | bytes accessed | tf_op | source)
XLA Modules:
  0.0 553.0 jit_solution(11055479898664694594)
XLA Ops:
  0.9 1.8 copy_multiply_fusion
  4.1 4.5 collective-permute-start
  8.6 1.3 collective-permute-done
  12.3 4.5 collective-permute-start.2
  20.5 1.9 broadcast_multiply_fusion
  23.8 4.8 collective-permute-start.4
  28.6 1.3 collective-permute-done.4
  31.1 1.4 copy.18
  34.1 4.8 collective-permute-start.6
  42.6 2.6 fusion.28
  46.6 4.8 collective-permute-start.8
  53.8 1.4 copy.22
  55.2 5.0 collective-permute-start.10
  62.3 5.0 collective-permute-done.11
  68.5 1.8 fusion.21
  71.6 4.9 collective-permute-start.12
  78.9 1.4 copy.26
  82.0 5.4 collective-permute-start.14
  91.1 8.3 %fusion.14 = f32[8,128,256]{2,0,1:T(8,128)S(1)} fusion(f32[8,128,256]{2,0,1:T(8,128)S(1)} %fusion.28, f32[8,128,256]{2,0,1:T(8,128)} %copy-done.1, f32[8,1,256]{2,0,1:T(8,128)S(1)} %collective-permute-done.12, f32[8,1,256]{2,0,1:T(8,128)S(1)} %collective-permute-done.13, f32[8,130,1]{2,0,1:T(8,128)} %copy.29, f32[8,130,1]{2,0,1:T(8,128)} %copy.27, ...), kind=kLoop, calls=%fused_computation.29 | loop fusion | flops 6815744 | bytes 5562516 | tf_op jit(solution)/shard_map/add | solution.py:60
  100.8 6.0 %collective-permute-start.16 = (f32[8,1,256]{2,0,1:T(8,128)S(1)}, f32[8,1,256]{2,0,1:T(8,128)S(1)}, u32[]{:S(2)}, u32[]{:S(2)}) collective-permute-start(f32[8,1,256]{2,0,1:T(8,128)S(1)} %get-tuple-element.18), channel_id=1, source_target_pairs={{0,32},{32,64},{64,96},{96,128},{128,160},{160,192},{192,224},{1,3... | collective-permute-start | bytes 24584 | tf_op jit(solution)/shard_map/ppermute | solution.py:13
  108.8 4.8 collective-permute-start.18
  114.0 1.5 collective-permute-start.19
  115.9 4.8 collective-permute-done.19
  121.9 1.8 fusion.5
  123.8 4.0 stack.19
  127.8 6.2 %all-to-all-start = ((f32[4,2,8,128,256]{4,2,3,1,0:T(8,128)}), f32[4,2,8,128,256]{4,2,3,1,0:T(8,128)}, u32[]{:S(2)}, u32[]{:S(2)}) async-start(f32[4,2,8,128,256]{4,2,3,1,0:T(8,128)} %stack.19), calls=%async_computation | async-start | bytes 16777216 | tf_op jit(solution)/shard_map/all_to_all | solution.py:68
  134.0 9.5 %reshape.17 = f32[64,32768,1]{1,0,2:T(8,128)} reshape(f32[64,128,256]{2,1,0:T(8,128)} %param.6) | data formatting | bytes 16777216 | tf_op jit(solution)/shard_map/reshape | solution.py:38
  143.4 82.1 %all-to-all-done = f32[4,2,8,128,256]{4,2,3,1,0:T(8,128)} async-done(((f32[4,2,8,128,256]{4,2,3,1,0:T(8,128)}), f32[4,2,8,128,256]{4,2,3,1,0:T(8,128)}, u32[]{:S(2)}, u32[]{:S(2)}) %all-to-all-start) | async-done | bytes 8388640 | tf_op jit(solution)/shard_map/all_to_all | solution.py:68
  225.5 4.1 copy.34
  229.7 1.7 copy-done
  231.3 6.8 %fusion.52 = f32[2,32,64]{2,1,0:T(8,128)S(1)} fusion(f32[2,32,32768]{2,1,0:T(8,128)S(1)} %bitcast.12, f32[64,32768,1]{1,0,2:T(8,128)S(1)} %copy-done), kind=kOutput, calls=%fused_computation.104 | convolution fusion | flops 1610612736 | bytes 16793600 | tf_op jit(solution)/shard_map/dot_general | solution.py:39
  238.1 314.3 %psum.7 = f32[2,32,64]{2,1,0:T(8,128)S(1)} all-reduce(f32[2,32,64]{2,1,0:T(8,128)S(1)} %fusion.52), channel_id=1, replica_groups=mesh['lx'=8,'ly'=8,'blk'=4] {'lx','ly'}, use_global_device_ids=true, to_apply=%region_0.1 | all-reduce | flops 4096 | bytes 32768 | tf_op jit(solution)/shard_map/psum | solution.py:72
  (70 shorter events, 37.3 us)
Async XLA Ops:
  2.8 5.9 %collective-permute-start.1 = (f32[8,1,256]{2,0,1:T(8,128)S(1)}, f32[8,1,256]{2,0,1:T(8,128)S(1)}, u32[]{:S(2)}, u32[]{:S(2)}) collective-permute-start(f32[8,1,256]{2,0,1:T(8,128)S(1)} %get-tuple-element.25), channel_id=1, source_target_pairs={{32,0},{64,32},{96,64},{128,96},{160,128},{192,160},{224,192},{33,... | collective-permute-start | bytes 24584 | tf_op jit(solution)/shard_map/ppermute | solution.py:16
  4.1 5.9 %collective-permute-start = (f32[8,1,256]{2,0,1:T(8,128)S(1)}, f32[8,1,256]{2,0,1:T(8,128)S(1)}, u32[]{:S(2)}, u32[]{:S(2)}) collective-permute-start(f32[8,1,256]{2,0,1:T(8,128)S(1)} %get-tuple-element.26), channel_id=1, source_target_pairs={{0,32},{32,64},{64,96},{96,128},{128,160},{160,192},{192,224},{1,3... | collective-permute-start | bytes 24584 | tf_op jit(solution)/shard_map/ppermute | solution.py:13
  10.3 10.3 %copy-start.2 = (f32[128,256]{1,0:T(8,128)S(1)}, f32[128,256]{1,0:T(8,128)}, u32[]{:S(2)}) copy-start(f32[128,256]{1,0:T(8,128)} %param.7) | copy-start | bytes 393220
  11.0 8.4 %collective-permute-start.3 = (f32[8,130,1]{1,0,2:T(8,128)S(1)}, f32[8,130,1]{1,0,2:T(8,128)S(1)}, u32[]{:S(2)}, u32[]{:S(2)}) collective-permute-start(f32[8,130,1]{1,0,2:T(8,128)S(1)} %copy.16), channel_id=1, source_target_pairs={{4,0},{8,4},{12,8},{16,12},{20,16},{24,20},{28,24},{5,1},{9,5},{13... | collective-permute-start | bytes 12488 | tf_op jit(solution)/shard_map/ppermute | solution.py:16
  12.3 5.9 %collective-permute-start.2 = (f32[8,130,1]{1,0,2:T(8,128)S(1)}, f32[8,130,1]{1,0,2:T(8,128)S(1)}, u32[]{:S(2)}, u32[]{:S(2)}) collective-permute-start(f32[8,130,1]{1,0,2:T(8,128)S(1)} %copy.14), channel_id=1, source_target_pairs={{0,4},{4,8},{8,12},{12,16},{16,20},{20,24},{24,28},{1,5},{5,9},{9,... | collective-permute-start | bytes 12488 | tf_op jit(solution)/shard_map/ppermute | solution.py:13
  22.5 6.1 %collective-permute-start.5 = (f32[8,1,256]{2,0,1:T(8,128)S(1)}, f32[8,1,256]{2,0,1:T(8,128)S(1)}, u32[]{:S(2)}, u32[]{:S(2)}) collective-permute-start(f32[8,1,256]{2,0,1:T(8,128)S(1)} %get-tuple-element.23), channel_id=1, source_target_pairs={{32,0},{64,32},{96,64},{128,96},{160,128},{192,160},{224,192},{33,... | collective-permute-start | bytes 24584 | tf_op jit(solution)/shard_map/ppermute | solution.py:16
  23.8 6.2 %collective-permute-start.4 = (f32[8,1,256]{2,0,1:T(8,128)S(1)}, f32[8,1,256]{2,0,1:T(8,128)S(1)}, u32[]{:S(2)}, u32[]{:S(2)}) collective-permute-start(f32[8,1,256]{2,0,1:T(8,128)S(1)} %get-tuple-element.24), channel_id=1, source_target_pairs={{0,32},{32,64},{64,96},{96,128},{128,160},{160,192},{192,224},{1,3... | collective-permute-start | bytes 24584 | tf_op jit(solution)/shard_map/ppermute | solution.py:13
  32.8 8.7 %collective-permute-start.7 = (f32[8,130,1]{1,0,2:T(8,128)S(1)}, f32[8,130,1]{1,0,2:T(8,128)S(1)}, u32[]{:S(2)}, u32[]{:S(2)}) collective-permute-start(f32[8,130,1]{1,0,2:T(8,128)S(1)} %copy.20), channel_id=1, source_target_pairs={{4,0},{8,4},{12,8},{16,12},{20,16},{24,20},{28,24},{5,1},{9,5},{13... | collective-permute-start | bytes 12488 | tf_op jit(solution)/shard_map/ppermute | solution.py:16
  34.1 6.2 %collective-permute-start.6 = (f32[8,130,1]{1,0,2:T(8,128)S(1)}, f32[8,130,1]{1,0,2:T(8,128)S(1)}, u32[]{:S(2)}, u32[]{:S(2)}) collective-permute-start(f32[8,130,1]{1,0,2:T(8,128)S(1)} %copy.18), channel_id=1, source_target_pairs={{0,4},{4,8},{8,12},{12,16},{16,20},{20,24},{24,28},{1,5},{5,9},{9,... | collective-permute-start | bytes 12488 | tf_op jit(solution)/shard_map/ppermute | solution.py:13
  45.3 6.1 %collective-permute-start.9 = (f32[8,1,256]{2,0,1:T(8,128)S(1)}, f32[8,1,256]{2,0,1:T(8,128)S(1)}, u32[]{:S(2)}, u32[]{:S(2)}) collective-permute-start(f32[8,1,256]{2,0,1:T(8,128)S(1)} %get-tuple-element.21), channel_id=1, source_target_pairs={{32,0},{64,32},{96,64},{128,96},{160,128},{192,160},{224,192},{33,... | collective-permute-start | bytes 24584 | tf_op jit(solution)/shard_map/ppermute | solution.py:16
  46.6 6.2 %collective-permute-start.8 = (f32[8,1,256]{2,0,1:T(8,128)S(1)}, f32[8,1,256]{2,0,1:T(8,128)S(1)}, u32[]{:S(2)}, u32[]{:S(2)}) collective-permute-start(f32[8,1,256]{2,0,1:T(8,128)S(1)} %get-tuple-element.22), channel_id=1, source_target_pairs={{0,32},{32,64},{64,96},{96,128},{128,160},{160,192},{192,224},{1,3... | collective-permute-start | bytes 24584 | tf_op jit(solution)/shard_map/ppermute | solution.py:13
  55.2 6.6 %collective-permute-start.10 = (f32[8,130,1]{1,0,2:T(8,128)S(1)}, f32[8,130,1]{1,0,2:T(8,128)S(1)}, u32[]{:S(2)}, u32[]{:S(2)}) collective-permute-start(f32[8,130,1]{1,0,2:T(8,128)S(1)} %copy.22), channel_id=1, source_target_pairs={{0,4},{4,8},{8,12},{12,16},{16,20},{20,24},{24,28},{1,5},{5,9},{9,... | collective-permute-start | bytes 12488 | tf_op jit(solution)/shard_map/ppermute | solution.py:13
  60.6 6.7 %collective-permute-start.11 = (f32[8,130,1]{1,0,2:T(8,128)S(1)}, f32[8,130,1]{1,0,2:T(8,128)S(1)}, u32[]{:S(2)}, u32[]{:S(2)}) collective-permute-start(f32[8,130,1]{1,0,2:T(8,128)S(1)} %copy.24), channel_id=1, source_target_pairs={{4,0},{8,4},{12,8},{16,12},{20,16},{24,20},{28,24},{5,1},{9,5},{13... | collective-permute-start | bytes 12488 | tf_op jit(solution)/shard_map/ppermute | solution.py:16
  70.3 7.7 %copy-start.1 = (f32[8,128,256]{2,0,1:T(8,128)}, f32[8,128,256]{2,0,1:T(8,128)S(1)}, u32[]{:S(2)}) copy-start(f32[8,128,256]{2,0,1:T(8,128)S(1)} %fusion.21) | copy-start | bytes 3145732
  70.3 6.2 %collective-permute-start.13 = (f32[8,1,256]{2,0,1:T(8,128)S(1)}, f32[8,1,256]{2,0,1:T(8,128)S(1)}, u32[]{:S(2)}, u32[]{:S(2)}) collective-permute-start(f32[8,1,256]{2,0,1:T(8,128)S(1)} %get-tuple-element.19), channel_id=1, source_target_pairs={{32,0},{64,32},{96,64},{128,96},{160,128},{192,160},{224,192},{33,... | collective-permute-start | bytes 24584 | tf_op jit(solution)/shard_map/ppermute | solution.py:16
  71.6 6.3 %collective-permute-start.12 = (f32[8,1,256]{2,0,1:T(8,128)S(1)}, f32[8,1,256]{2,0,1:T(8,128)S(1)}, u32[]{:S(2)}, u32[]{:S(2)}) collective-permute-start(f32[8,1,256]{2,0,1:T(8,128)S(1)} %get-tuple-element.20), channel_id=1, source_target_pairs={{0,32},{32,64},{64,96},{96,128},{128,160},{160,192},{192,224},{1,3... | collective-permute-start | bytes 24584 | tf_op jit(solution)/shard_map/ppermute | solution.py:13
  78.9 8.5 %copy-start.3 = (f32[5]{0:T(128)S(1)}, f32[5]{0:T(128)}, u32[]{:S(2)}) copy-start(f32[5]{0:T(128)} %param.9) | copy-start | bytes 64
  80.7 9.3 %collective-permute-start.15 = (f32[8,130,1]{1,0,2:T(8,128)S(1)}, f32[8,130,1]{1,0,2:T(8,128)S(1)}, u32[]{:S(2)}, u32[]{:S(2)}) collective-permute-start(f32[8,130,1]{1,0,2:T(8,128)S(1)} %copy.28), channel_id=1, source_target_pairs={{4,0},{8,4},{12,8},{16,12},{20,16},{24,20},{28,24},{5,1},{9,5},{13... | collective-permute-start | bytes 12488 | tf_op jit(solution)/shard_map/ppermute | solution.py:16
  82.0 6.8 %collective-permute-start.14 = (f32[8,130,1]{1,0,2:T(8,128)S(1)}, f32[8,130,1]{1,0,2:T(8,128)S(1)}, u32[]{:S(2)}, u32[]{:S(2)}) collective-permute-start(f32[8,130,1]{1,0,2:T(8,128)S(1)} %copy.26), channel_id=1, source_target_pairs={{0,4},{4,8},{8,12},{12,16},{16,20},{20,24},{24,28},{1,5},{5,9},{9,... | collective-permute-start | bytes 12488 | tf_op jit(solution)/shard_map/ppermute | solution.py:13
  99.5 7.3 %collective-permute-start.17 = (f32[8,1,256]{2,0,1:T(8,128)S(1)}, f32[8,1,256]{2,0,1:T(8,128)S(1)}, u32[]{:S(2)}, u32[]{:S(2)}) collective-permute-start(f32[8,1,256]{2,0,1:T(8,128)S(1)} %get-tuple-element.17), channel_id=1, source_target_pairs={{32,0},{64,32},{96,64},{128,96},{160,128},{192,160},{224,192},{33,... | collective-permute-start | bytes 24584 | tf_op jit(solution)/shard_map/ppermute | solution.py:16
  100.8 7.4 %collective-permute-start.16 = (f32[8,1,256]{2,0,1:T(8,128)S(1)}, f32[8,1,256]{2,0,1:T(8,128)S(1)}, u32[]{:S(2)}, u32[]{:S(2)}) collective-permute-start(f32[8,1,256]{2,0,1:T(8,128)S(1)} %get-tuple-element.18), channel_id=1, source_target_pairs={{0,32},{32,64},{64,96},{96,128},{128,160},{160,192},{192,224},{1,3... | collective-permute-start | bytes 24584 | tf_op jit(solution)/shard_map/ppermute | solution.py:13
  108.8 6.7 %collective-permute-start.18 = (f32[8,130,1]{1,0,2:T(8,128)S(1)}, f32[8,130,1]{1,0,2:T(8,128)S(1)}, u32[]{:S(2)}, u32[]{:S(2)}) collective-permute-start(f32[8,130,1]{1,0,2:T(8,128)S(1)} %copy.30), channel_id=1, source_target_pairs={{0,4},{4,8},{8,12},{12,16},{16,20},{20,24},{24,28},{1,5},{5,9},{9,... | collective-permute-start | bytes 12488 | tf_op jit(solution)/shard_map/ppermute | solution.py:13
  114.0 6.7 %collective-permute-start.19 = (f32[8,130,1]{1,0,2:T(8,128)S(1)}, f32[8,130,1]{1,0,2:T(8,128)S(1)}, u32[]{:S(2)}, u32[]{:S(2)}) collective-permute-start(f32[8,130,1]{1,0,2:T(8,128)S(1)} %copy.32), channel_id=1, source_target_pairs={{4,0},{8,4},{12,8},{16,12},{20,16},{24,20},{28,24},{5,1},{9,5},{13... | collective-permute-start | bytes 12488 | tf_op jit(solution)/shard_map/ppermute | solution.py:16
  127.8 97.8 %all-to-all-start = ((f32[4,2,8,128,256]{4,2,3,1,0:T(8,128)}), f32[4,2,8,128,256]{4,2,3,1,0:T(8,128)}, u32[]{:S(2)}, u32[]{:S(2)}) async-start(f32[4,2,8,128,256]{4,2,3,1,0:T(8,128)} %stack.19), calls=%async_computation | async-start | bytes 16777216 | tf_op jit(solution)/shard_map/all_to_all | solution.py:68
  225.5 5.8 %copy-start = (f32[64,32768,1]{1,0,2:T(8,128)S(1)}, f32[64,32768,1]{1,0,2:T(8,128)}, u32[]{:S(2)}) copy-start(f32[64,32768,1]{1,0,2:T(8,128)} %reshape.17) | copy-start | bytes 25165828
